TPU v7x, 128 devices: a whole 4x4x4 slice. The times are simulated.
128 devices in a mesh: row: 8 (over z, core), col: 16 (over y, x).
Axes of the slice: x: 4, y: 4, z: 4, core: 2. Of those that a mesh axis runs over, the one named last changes fastest.
Arguments:
- panel_blocks: bfloat16 [16, 8, 512, 512], P('col', None, 'row'), may hold values from -0.25 to 0.25
- factor_inverse: bfloat16 [16, 512, 512], P('col')
- target_rows: int32 [16, 8], replicated, may hold values from 0 to 15, as said below
- owner_order: int32 [16], replicated, may hold values from 0 to 15, each once
- ancestor_rows: float32 [16, 512, 8192], P('col', 'row'), may hold values from -1.8 to 1.8
Outputs:
- updated_rows: float32 [16, 512, 8192], P('col', 'row')
Inputs may be any that keep to these rules, and one draw needn't show every extreme that they name: `target_rows`: each row names 8 different ancestor block rows in ascending order; each index of col holds exactly one supernode. `owner_order`: each ancestor block row once.
All inputs are finite; a program needn't handle non-finite values.
Results may differ from a plain program's by a relative error of at most 0.0024.
Values may be sent and summed in bfloat16 or wider, within the bound.
A program may use at most 192 MiB of HBM per device.

v0:
```python
import jax
import jax.numpy as jnp
from jax import lax
from jax.sharding import PartitionSpec as P


def solve_rows(blocks, factor_inverse):
    return jnp.einsum(
        "spiw,svw->spiv", blocks, factor_inverse, preferred_element_type=jnp.float32
    ).astype(jnp.bfloat16)


def pick_rows(products, own_targets, order_part):
    matched = own_targets[None, :, :] == order_part[:, None, None]
    places = lax.broadcasted_iota(jnp.int32, matched.shape, 2)
    position = jnp.sum(jnp.where(matched, places, 0), axis=2)
    present = jnp.any(matched, axis=2)
    supernode_ids = lax.broadcasted_iota(jnp.int32, position.shape, 1)
    chosen = products[supernode_ids, position]
    return jnp.where(present[:, :, None, None, None], chosen, jnp.zeros((), chosen.dtype))


def body(panel_blocks, factor_inverse, target_rows, owner_order, ancestor_rows):
    supernodes = panel_blocks.shape[0]
    own_height = panel_blocks.shape[2]
    width = panel_blocks.shape[3]
    ancestors = owner_order.shape[0]
    col_place = lax.axis_index("col")
    own_targets = lax.dynamic_slice_in_dim(target_rows, col_place * supernodes, supernodes, 0)
    own_solved = solve_rows(panel_blocks, factor_inverse)
    products = jnp.einsum(
        "spiw,sqmw->spiqm",
        own_solved,
        lax.all_gather(own_solved, "row", axis=2, tiled=True),
        preferred_element_type=jnp.float32,
    ).astype(jnp.bfloat16)
    block_ids = lax.broadcasted_iota(jnp.int32, (1, 1, 1, ancestors), 3)
    own_onehot = (own_targets[:, :, None] == block_ids[0]).astype(jnp.bfloat16)
    chosen = pick_rows(products, own_targets, owner_order)
    spread = jnp.einsum("sqb,jsiqw->jibw", own_onehot, chosen, preferred_element_type=jnp.float32)
    summed = lax.psum_scatter(
        spread.reshape(
            ancestor_rows.shape[0] * lax.axis_size("col"), own_height, ancestors * width
        ),
        "col",
        scatter_dimension=0,
        tiled=True,
    )
    return ancestor_rows - summed


def solution(mesh):
    return jax.shard_map(
        body,
        mesh=mesh,
        in_specs=(
            P("col", None, "row", None),
            P("col", None, None),
            P(),
            P(),
            P("col", "row", None),
        ),
        out_specs=P("col", "row", None),
        check_vma=False,
    )
```

profile of v0, /device:TPU:1, one launch (start us, length us, event | category | flops | bytes accessed | tf_op | source)
XLA Modules:
  0.0 327.5 jit_solution(10191502747342464816)
XLA Ops:
  6.5 0.0 copy-start
  6.5 0.0 all-gather.3.cloned.1.call-start
  6.5 1.0 copy-done
  7.6 2.3 convolution_convert_fusion
  9.9 0.0 all-gather.3.cloned.1.call-update
  9.9 0.0 reduce-scatter.4.cloned.1.call-start
  10.0 0.9 dynamic-slice_reduce_fusion
  10.8 0.7 fusion.9
  11.6 0.7 compare_reduce_fusion
  12.3 33.7 %all-gather.3.cloned.1.call-done = bf16[8,512,512]{2,1,0:T(8,128)(2,1)} async-done(((bf16[8,64,512]{2,1,0:T(8,128)(2,1)}), bf16[8,512,512]{2,1,0:T(8,128)(2,1)}) %all-gather.3.cloned.1.call-update) | async-done | bytes 4194320 | tf_op jit(solution)/shard_map/all_gather | solution.py:34
  46.1 6.7 %convert_bitcast_fusion = bf16[1,8,64,8,512]{4,2,3,1,0:T(8,128)(2,1)} fusion(bf16[8,512,512]{2,1,0:T(8,128)(2,1)} %all-gather.3.cloned.1.call-done, bf16[8,64,512]{2,1,0:T(8,128)(2,1)} %convolution_convert_fusion), kind=kOutput, calls=%fused_computation.7 | convolution fusion | flops 2149580800 | bytes 8912896 | tf_op jit(solution)/shard_map/spiw,sqmw->spiqm/dot_general | solution.py:31
  52.7 6.9 %gather_fusion = bf16[16,64,8,512]{3,1,2,0:T(8,128)(2,1)} fusion(bf16[1,8,64,8,512]{4,2,3,1,0:T(8,128)(2,1)} %convert_bitcast_fusion, s32[16]{0:T(128)S(1)} %or_bitcast_fusion), kind=kCustom, calls=%fused_computation | custom fusion | bytes 16777344 | tf_op jit(solution)/shard_map/gather | solution.py:19
  59.6 7.2 %fusion = bf16[16,64,8,512]{3,1,2,0:T(8,128)(2,1)} fusion(bf16[16,64,8,512]{3,1,2,0:T(8,128)(2,1)} %gather_fusion, pred[16]{0:T(512)(128)(4,1)S(1)} %compare_reduce_fusion), kind=kLoop, calls=%fused_computation.3 | loop fusion | flops 4194304 | bytes 16777232 | tf_op jit(solution)/shard_map/jit(_where)/select_n | solution.py:20
  66.8 20.6 %convolution_bitcast_fusion = f32[16,64,16,512]{3,2,1,0:T(8,128)} fusion(bf16[16,64,8,512]{3,1,2,0:T(8,128)(2,1)} %fusion, s32[8]{0:T(128)S(1)} %dynamic-slice_reduce_fusion), kind=kOutput, calls=%fused_computation.1 | convolution fusion | flops 134217856 | bytes 41943072 | tf_op jit(solution)/shard_map/sqb,jsiqw->jibw/dot_general | solution.py:40
  87.4 35.9 %reshape.219 = f32[16,64,8192]{2,1,0:T(8,128)} reshape(f32[16,64,16,512]{3,2,1,0:T(8,128)} %convolution_bitcast_fusion) | data formatting | bytes 67108864 | tf_op jit(solution)/shard_map/reshape | solution.py:42
  123.3 0.0 copy-start.2
  123.3 0.0 reduce-scatter.4.cloned.1.call-update
  123.3 0.0 copy-start.1
  123.3 194.2 %reduce-scatter.4.cloned.1.call-done = f32[1,64,8192]{2,1,0:T(8,128)} async-done(((f32[16,64,8192]{2,1,0:T(8,128)}), f32[1,64,8192]{2,1,0:T(8,128)}) %reduce-scatter.4.cloned.1.call-update) | async-done | bytes 2097168
  317.5 0.0 copy-done.2
  317.5 3.1 sub.3
  320.7 0.0 copy-done.1
  (3 shorter events, 0.0 us)
Async XLA Ops:
  6.5 1.0 copy-start
  6.5 39.5 %all-gather.3.cloned.1.call-start = ((), (), s32[]{:S(2)}) async-start(), calls=%async_computation.1 | async-start | bytes 4718592 | tf_op jit(solution)/shard_map/all_gather | solution.py:34
  9.9 307.6 %reduce-scatter.4.cloned.1.call-start = ((), (), s32[]{:S(2)}) async-start(), calls=%async_computation.2 | async-start | bytes 35651584
  123.3 194.3 %copy-start.2 = (f32[1,64,8192]{2,1,0:T(8,128)S(1)}, f32[1,64,8192]{2,1,0:T(8,128)}, u32[]{:S(2)}) copy-start(f32[1,64,8192]{2,1,0:T(8,128)} %param.9) | copy-start | bytes 6291460
  123.3 197.4 %copy-start.1 = (bf16[1,512,512]{2,1,0:T(8,128)(2,1)S(1)}, bf16[1,512,512]{2,1,0:T(8,128)(2,1)}, u32[]{:S(2)}) copy-start(bf16[1,512,512]{2,1,0:T(8,128)(2,1)} %param.6) | copy-start | bytes 1572868
Sparse Core Ops, SparseCore 0:
  10.0 35.9 all-gather.2
  123.4 194.0 reduce-scatter.3
where the time goes:
time: 329 us; the launch traced here: 328 us
  waiting for transfers between devices  228 us (69%)
  local copies, waits for them, and re-layouts  44.7 us (14%)
  matrix products  29.6 us (9%)
  between operations  13.4 us (4%)
  other arithmetic  11.8 us (4%)
    unnamed x3, waiting for transfers between devices  194 us
    reshape x1, local copies, waits for them, and re-layouts, body(): spread.reshape(ancestor_rows.shape[0] * lax.axis_size('col'), own_height,...  35.9 us
    all_gather x1, waiting for transfers between devices, body(): lax.all_gather(own_solved, 'row', axis=2, tiled=True)  33.7 us
    dot_general x1, matrix products, body(): jnp.einsum('sqb,jsiqw->jibw', own_onehot, chosen, preferred_element_type=...  20.6 us
    select_n x1, other arithmetic, pick_rows(): jnp.where(present[:, :, None, None, None], chosen, jnp.zeros((), chosen.d...  7.19 us
    gather x1, local copies, waits for them, and re-layouts, pick_rows(): chosen = products[supernode_ids, position]  6.87 us
    dot_general x1, matrix products, body(): jnp.einsum('spiw,sqmw->spiqm', own_solved, lax.all_gather(own_solved, 'ro...  6.66 us
  transfers between devices with their start and end apart: 2, of which 2 were waited for; matrix products, arithmetic and copies ran while one was open for 1% of the time, Pallas kernels for 0%

commit v1 on v0

v1 whole, which is shorter than its diff:
```python
import jax
import jax.numpy as jnp
from jax import lax
from jax.sharding import PartitionSpec as P


def body(panel_blocks, factor_inverse, target_rows, owner_order, ancestor_rows):
    col_size = lax.axis_size("col")
    width = panel_blocks.shape[3]
    ancestors = owner_order.shape[0]
    col_place = lax.axis_index("col")
    own_targets = lax.dynamic_slice_in_dim(target_rows, col_place, 1, 0)[0]
    own_solved = jnp.einsum(
        "piw,vw->piv", panel_blocks[0], factor_inverse[0], preferred_element_type=jnp.float32
    ).astype(jnp.bfloat16)
    full_solved = lax.all_gather(own_solved, "row", axis=1, tiled=True)
    products = jnp.einsum(
        "piw,qmw->piqm", own_solved, full_solved, preferred_element_type=jnp.float32
    ).astype(jnp.bfloat16)
    matched = own_targets[None, :] == owner_order[:, None]
    places = lax.broadcasted_iota(jnp.int32, matched.shape, 1)
    position = jnp.sum(jnp.where(matched, places, 0), axis=1)
    present = jnp.any(matched, axis=1)
    send = jnp.where(present[:, None, None, None], products[position], jnp.zeros((), products.dtype))
    received = lax.all_to_all(send, "col", 0, 0, tiled=True)
    block_ids = lax.broadcasted_iota(jnp.int32, (1, 1, ancestors), 2)
    onehot = (target_rows[:, :, None] == block_ids).astype(jnp.bfloat16)
    update = jnp.einsum("sqb,siqm->ibm", onehot, received, preferred_element_type=jnp.float32)
    return ancestor_rows - update.reshape(ancestor_rows.shape)


def solution(mesh):
    return jax.shard_map(
        body,
        mesh=mesh,
        in_specs=(
            P("col", None, "row", None),
            P("col", None, None),
            P(),
            P(),
            P("col", "row", None),
        ),
        out_specs=P("col", "row", None),
        check_vma=False,
    )
```

time: 329 us -> 219 us (0.67)
  waiting for transfers between devices: 228 us -> 159 us
  local copies, waits for them, and re-layouts: 44.7 us -> 15.1 us
  matrix products: 29.6 us -> 13 us
  starting transfers between devices: 0.04 us -> 6.71 us
    unnamed x3 -> x1, waiting for transfers between devices: 194 us -> 0.02 us
    all_to_all x0 -> x1, waiting for transfers between devices: none -> 125 us  [body(): received = lax.all_to_all(send, 'col', 0, 0, tiled=True)]
    reshape x1, local copies, waits for them, and re-layouts: 35.9 us -> 1.75 us  [body(): return ancestor_rows - update.reshape(ancestor_rows.shape)]
    dot_general x3, matrix products: 29.6 us -> 13 us  [the longest x1 6.02 us: body(): jnp.einsum('sqb,siqm->ibm', onehot, received, preferred_element_type=jnp....]
    all_to_all x0 -> x1, starting transfers between devices: none -> 6.71 us  [body(): received = lax.all_to_all(send, 'col', 0, 0, tiled=True)]
    convert_element_type x0 -> x1, local copies, waits for them, and re-layouts: none -> 4.47 us  [body(): products = jnp.einsum('piw,qmw->piqm', own_solved, full_solved, preferred...]
where the time goes in v1:
time: 219 us
  waiting for transfers between devices  159 us (73%)
  local copies, waits for them, and re-layouts  15.1 us (7%)
  between operations  13.4 us (6%)
  matrix products  13 us (6%)
  other arithmetic  11.8 us (5%)
  starting transfers between devices  6.71 us (3%)
    all_to_all x1, waiting for transfers between devices, body(): received = lax.all_to_all(send, 'col', 0, 0, tiled=True)  125 us
    all_gather x1, waiting for transfers between devices, body(): full_solved = lax.all_gather(own_solved, 'row', axis=1, tiled=True)  33.7 us
    select_n x1, other arithmetic, body(): jnp.where(present[:, None, None, None], products[position], jnp.zeros((),...  7.2 us
    gather x1, local copies, waits for them, and re-layouts, body(): products[position]  6.87 us
    all_to_all x1, starting transfers between devices, body(): received = lax.all_to_all(send, 'col', 0, 0, tiled=True)  6.71 us
    dot_general x1, matrix products, body(): jnp.einsum('sqb,siqm->ibm', onehot, received, preferred_element_type=jnp....  6.02 us
    dot_general x1, matrix products, body(): jnp.einsum('piw,qmw->piqm', own_solved, full_solved, preferred_element_ty...  4.73 us
    convert_element_type x1, local copies, waits for them, and re-layouts, body(): products = jnp.einsum('piw,qmw->piqm', own_solved, full_solved, preferred...  4.47 us
  transfers between devices with their start and end apart: 2, of which 2 were waited for; matrix products, arithmetic and copies ran while one was open for 1% of the time, Pallas kernels for 0%

profile of v1, /device:TPU:1, one launch (start us, length us, event | category | flops | bytes accessed | tf_op | source)
XLA Modules:
  0.0 218.7 jit_solution(13225717698894345203)
XLA Ops:
  6.5 0.0 copy-start
  6.5 0.0 all-gather.2.cloned.1.call-start
  6.5 1.0 copy-done
  7.6 2.3 %convolution_convert_fusion = bf16[8,64,512]{2,1,0:T(8,128)(2,1)} fusion(bf16[1,512,512]{2,1,0:T(8,128)(2,1)S(1)} %copy-done, bf16[1,8,64,512]{3,2,1,0:T(8,128)(2,1)} %param.5), kind=kOutput, calls=%fused_computation.6 | convolution fusion | flops 268697600 | bytes 1572864 | tf_op jit(solution)/shard_map/piw,vw->piv/dot_general | solution.py:13
  9.9 0.0 all-gather.2.cloned.1.call-update
  9.9 0.9 dynamic-slice_reduce_fusion
  10.8 0.7 fusion.11
  11.5 0.7 compare_reduce_fusion
  12.3 33.7 %all-gather.2.cloned.1.call-done = bf16[8,512,512]{2,1,0:T(8,128)(2,1)} async-done(((bf16[8,64,512]{2,1,0:T(8,128)(2,1)}), bf16[8,512,512]{2,1,0:T(8,128)(2,1)}) %all-gather.2.cloned.1.call-update) | async-done | bytes 4194320 | tf_op jit(solution)/shard_map/all_gather | solution.py:16
  46.0 4.7 %fusion.2 = bf16[8,64,8,512]{3,1,2,0:T(8,128)(2,1)S(1)} fusion(bf16[8,512,512]{2,1,0:T(8,128)(2,1)} %all-gather.2.cloned.1.call-done, bf16[8,64,512]{2,1,0:T(8,128)(2,1)} %convolution_convert_fusion), kind=kOutput, calls=%fused_computation.4 | convolution fusion | flops 2149580800 | bytes 8912896 | tf_op jit(solution)/shard_map/piw,qmw->piqm/dot_general | solution.py:17
  50.8 4.5 %copy.9 = bf16[8,64,8,512]{3,2,1,0:T(8,128)(2,1)} copy(bf16[8,64,8,512]{3,1,2,0:T(8,128)(2,1)S(1)} %fusion.2) | data formatting | bytes 8388608 | tf_op jit(solution)/shard_map/convert_element_type | solution.py:19
  55.2 6.9 %gather_fusion = bf16[16,64,8,512]{3,2,1,0:T(8,128)(2,1)} fusion(bf16[8,64,8,512]{3,2,1,0:T(8,128)(2,1)} %copy.9, s32[1024]{0:T(1024)S(1)} %pad_clamp_fusion), kind=kCustom, calls=%fused_computation | custom fusion | bytes 16777280 | tf_op jit(solution)/shard_map/gather | solution.py:24
  62.1 7.2 %broadcast_select_fusion = bf16[16,64,8,512]{3,2,1,0:T(8,128)(2,1)} fusion(bf16[16,64,8,512]{3,2,1,0:T(8,128)(2,1)} %gather_fusion, pred[16]{0:T(512)(128)(4,1)S(1)} %compare_reduce_fusion), kind=kLoop, calls=%fused_computation.1 | loop fusion | flops 4194304 | bytes 16777232 | tf_op jit(solution)/shard_map/jit(_where)/select_n | solution.py:24
  69.3 0.0 copy-start.1
  69.3 6.7 %all-to-all-start = ((bf16[16,64,8,512]{3,2,1,0:T(8,128)(2,1)}), bf16[16,64,8,512]{3,2,1,0:T(8,128)(2,1)}, u32[]{:S(2)}, u32[]{:S(2)}) async-start(bf16[16,64,8,512]{3,2,1,0:T(8,128)(2,1)} %broadcast_select_fusion), calls=%async_computation | async-start | bytes 16777216 | tf_op jit(solution)/shard_map/all_to_all | solution.py:25
  76.0 0.0 copy-done.1
  76.0 0.1 copy.10
  76.1 124.9 %all-to-all-done = bf16[16,64,8,512]{3,2,1,0:T(8,128)(2,1)} async-done(((bf16[16,64,8,512]{3,2,1,0:T(8,128)(2,1)}), bf16[16,64,8,512]{3,2,1,0:T(8,128)(2,1)}, u32[]{:S(2)}, u32[]{:S(2)}) %all-to-all-start) | async-done | bytes 8388640 | tf_op jit(solution)/shard_map/all_to_all | solution.py:25
  201.0 6.0 %convolution_bitcast_fusion = f32[64,16,512]{2,1,0:T(8,128)} fusion(bf16[16,64,8,512]{3,2,1,0:T(8,128)(2,1)} %all-to-all-done, s32[16,8]{1,0:T(8,128)S(1)} %copy.10), kind=kOutput, calls=%fused_computation.5 | convolution fusion | flops 134219776 | bytes 10486272 | tf_op jit(solution)/shard_map/sqb,siqm->ibm/dot_general | solution.py:28
  207.0 1.7 reshape.19
  208.7 3.1 %sub.3 = f32[1,64,8192]{2,1,0:T(8,128)} subtract(f32[1,64,8192]{2,1,0:T(8,128)} %param.9, f32[1,64,8192]{2,1,0:T(8,128)S(1)} %reshape.19) | non-fusion elementwise | flops 524288 | bytes 6291456 | tf_op jit(solution)/shard_map/sub | solution.py:29
  (2 shorter events, 0.0 us)
Async XLA Ops:
  6.5 1.0 copy-start
  6.5 39.5 %all-gather.2.cloned.1.call-start = ((), (), s32[]{:S(2)}) async-start(), calls=%async_computation.1 | async-start | bytes 4718592 | tf_op jit(solution)/shard_map/all_gather | solution.py:16
  69.3 6.7 %copy-start.1 = (s32[16,8]{0,1:T(8,128)S(1)}, s32[16,8]{0,1:T(8,128)}, u32[]{:S(2)}) copy-start(s32[16,8]{0,1:T(8,128)} %param.7) | copy-start | bytes 1540
  69.3 131.7 %all-to-all-start = ((bf16[16,64,8,512]{3,2,1,0:T(8,128)(2,1)}), bf16[16,64,8,512]{3,2,1,0:T(8,128)(2,1)}, u32[]{:S(2)}, u32[]{:S(2)}) async-start(bf16[16,64,8,512]{3,2,1,0:T(8,128)(2,1)} %broadcast_select_fusion), calls=%async_computation | async-start | bytes 16777216 | tf_op jit(solution)/shard_map/all_to_all | solution.py:25
Sparse Core Ops, SparseCore 0:
  10.0 35.9 all-gather.1
